TPU v7x, 512 devices: a whole 4x8x8 slice. The times are simulated.
512 devices in a mesh: sims: 32 (over z_lo, y, core), rows: 16 (over x, z_hi).
Axes of the slice: x: 4, y: 8, z: 8 (z_hi: 4, z_lo: 2; z = z_hi * 2 + z_lo), core: 2. Of those that a mesh axis runs over, the one named last changes fastest.
Arguments:
- maps: float32 [32, 1024, 2048], P('sims', 'rows'), may hold values from -6 to 6
- weight: float32 [1024, 2048], P('rows'), may hold values from 0.1 to 1.5
- beam: float32 [65], replicated, may hold values from 0.05 to 1
- pair_one: int32 [32], replicated, may hold values from 0 to 31, each once
- pair_two: int32 [32], replicated, may hold values from 0 to 31, each once
- owner: int32 [32], replicated, may hold values from 0 to 7
Outputs:
- estimate: float32 [32, 1024, 2048], P('sims', 'rows')
- mean_field: float32 [8, 1024, 2048], P(None, 'rows', 'sims')
Inputs may be any that keep to these rules, and one draw needn't show every extreme that they name: `pair_one`: each a permutation of the evolutions. `pair_two`: each a permutation of the evolutions.
All inputs are finite; a program needn't handle non-finite values.
Results may differ from a plain program's by a relative error of at most 0.00016.
Values sent between devices are 32-bit elements; how exact they have to be, the bound alone decides.
A program may use at most 64 MiB of HBM per device.

v0:
```python
import jax
import jax.numpy as jnp
from jax import lax
from jax.experimental import pallas as pl
from jax.experimental.pallas import tpu as pltpu
from jax.sharding import Mesh
from jax.sharding import PartitionSpec as P

TAPS = 65
ITERS = 3
OWNERS = 8
STEPS = 2 * ITERS + 1
REACH = 32
LANES = 128
WIDE = 256
WINDOW = 512
ridge_term = 0.5
step_size = 0.6
F32 = jnp.float32
BF16 = jnp.bfloat16
MESH = pl.DeviceIdType.MESH


def halves(x):
    high = x.astype(BF16)
    return high, (x - high.astype(F32)).astype(BF16)


def dot(a, b):
    return jnp.dot(a, b, preferred_element_type=F32)


def filter_kernel(maps_ref, weight_ref, taps_ref, out_ref, f_ref, source_ref, h_ref, acc_ref, top_ref, bottom_ref, rim_out, rim_in, across_h, across_l, down_own, down_rim, x_h, x_l, own_ref, rim_ref, edge_ref, send_sem, recv_sem, rim_send, rim_recv):
    count = lax.axis_size("rows")
    me = lax.axis_index("rows")
    above, below = {"rows": me - 1}, {"rows": me + 1}
    has_above, has_below = me > 0, me < count - 1
    rows, cols = f_ref.shape
    blocks, pairs = cols // LANES, cols // WIDE

    barrier = pltpu.get_barrier_semaphore()

    @pl.when(has_above)
    def _():
        pl.semaphore_signal(barrier, inc=1, device_id=above, device_id_type=MESH)

    @pl.when(has_below)
    def _():
        pl.semaphore_signal(barrier, inc=1, device_id=below, device_id_type=MESH)

    for way in range(2):
        line = jnp.broadcast_to(taps_ref[1 - way : 2 - way, :], (WINDOW, WINDOW))
        table = pltpu.roll(line, WINDOW - 160, 1, stride=1, stride_axis=0)[:, :WIDE]
        high, low = halves(table)
        across_h[way] = high
        across_l[way] = low
        line = jnp.broadcast_to(taps_ref[way : way + 1, :LANES], (rows, LANES))
        inside = pltpu.roll(line, LANES - REACH, 1, stride=1, stride_axis=0)
        over = pltpu.roll(line, 64, 1, stride=1, stride_axis=0)
        under = pltpu.roll(line, 0, 1, stride=1, stride_axis=0)
        place = lax.broadcasted_iota(jnp.int32, (rows, LANES), 1)
        rim = jnp.where(place < 96, over, under)
        high, low = halves(inside[:, :64])
        down_own[way] = jnp.concatenate([high, low, high], axis=1)
        high, low = halves(rim[:, 64:])
        down_rim[way] = jnp.concatenate([high, low, high], axis=1)

    nothing = jnp.zeros((rows, LANES), BF16)
    for ref in (x_h, x_l):
        ref[0:rows, 0:LANES] = nothing
        ref[(pairs - 1) * rows : pairs * rows, 3 * LANES : 4 * LANES] = nothing

    @pl.when(jnp.logical_not(has_above))
    def _():
        top_ref[...] = jnp.zeros_like(top_ref)
        rim_in[0] = jnp.zeros_like(rim_in[0])

    @pl.when(jnp.logical_not(has_below))
    def _():
        bottom_ref[...] = jnp.zeros_like(bottom_ref)
        rim_in[1] = jnp.zeros_like(rim_in[1])

    def put(block, value):
        high, low = halves(value)
        for pair in range(pairs):
            place = block - 2 * pair + 1
            if 0 <= place < 4:
                spot = (slice(pair * rows, (pair + 1) * rows), slice(place * LANES, (place + 1) * LANES))
                x_h[spot] = high
                x_l[spot] = low

    def up_copy(step):
        return pltpu.make_async_remote_copy(
            src_ref=h_ref.at[0:REACH], dst_ref=bottom_ref.at[step], send_sem=send_sem.at[0, step], recv_sem=recv_sem.at[1, step], device_id=above, device_id_type=MESH
        )

    def down_copy(step):
        return pltpu.make_async_remote_copy(
            src_ref=h_ref.at[REACH : 2 * REACH], dst_ref=top_ref.at[step], send_sem=send_sem.at[1, step], recv_sem=recv_sem.at[0, step], device_id=below, device_id_type=MESH
        )

    def half_step(step, way):
        table_h, table_l = across_h[way], across_l[way]
        for pair in range(pairs):
            high, low = x_h[pair * rows : (pair + 1) * rows], x_l[pair * rows : (pair + 1) * rows]
            both = dot(jnp.concatenate([high, low], axis=0), table_h)
            value = both[:rows] + both[rows:] + dot(high, table_l)
            h_ref[:, pair * WIDE : (pair + 1) * WIDE] = value

        @pl.when(has_above)
        def _():
            up_copy(step).start()

        @pl.when(has_below)
        def _():
            down_copy(step).start()

        high, low = halves(h_ref[...])
        own_ref[0:rows] = high
        own_ref[rows : 2 * rows] = high
        own_ref[2 * rows : 3 * rows] = low
        acc_ref[...] = dot(down_own[way], own_ref[...])

        @pl.when(has_above)
        def _():
            down_copy(step).wait_recv()

        @pl.when(has_below)
        def _():
            up_copy(step).wait_recv()

        for at, ref in ((0, top_ref), (REACH, bottom_ref)):
            high, low = halves(ref[step])
            rim_ref[at : at + REACH] = high
            rim_ref[rows + at : rows + at + REACH] = high
            rim_ref[2 * rows + at : 2 * rows + at + REACH] = low
        acc_ref[...] += dot(down_rim[way], rim_ref[...])

        @pl.when(has_above)
        def _():
            up_copy(step).wait_send()

        @pl.when(has_below)
        def _():
            down_copy(step).wait_send()

    spans = [slice(b * LANES, (b + 1) * LANES) for b in range(blocks)]
    for b in range(blocks):
        put(b, weight_ref[:, spans[b]] * maps_ref[:, spans[b]])

    inner = jnp.logical_and(has_above, has_below)

    @pl.when(inner)
    def _():
        pl.semaphore_wait(barrier, 2)

    @pl.when(jnp.logical_not(inner))
    def _():
        pl.semaphore_wait(barrier, 1)

    half_step(0, 1)
    for b in range(blocks):
        first = step_size * acc_ref[:, spans[b]]
        source_ref[:, spans[b]] = first
        f_ref[:, spans[b]] = first
        put(b, first)

    def iteration(turn, carry):
        half_step(2 * turn + 1, 0)
        for b in range(blocks):
            put(b, weight_ref[:, spans[b]] * acc_ref[:, spans[b]])
        half_step(2 * turn + 2, 1)
        for b in range(blocks):
            value = (1.0 - step_size * ridge_term) * f_ref[:, spans[b]] + source_ref[:, spans[b]] - step_size * acc_ref[:, spans[b]]
            f_ref[:, spans[b]] = value
            put(b, value)
        return carry

    lax.fori_loop(0, ITERS, iteration, 0)

    quarter = cols // 4
    for k in range(4):
        rim_out[0, 2 * k : 2 * k + 2, :] = f_ref[0:2, k * quarter : (k + 1) * quarter]
        rim_out[1, 2 * k : 2 * k + 2, :] = f_ref[rows - 2 : rows, k * quarter : (k + 1) * quarter]

    def rim_up():
        return pltpu.make_async_remote_copy(src_ref=rim_out.at[0], dst_ref=rim_in.at[1], send_sem=rim_send.at[0], recv_sem=rim_recv.at[1], device_id=above, device_id_type=MESH)

    def rim_down():
        return pltpu.make_async_remote_copy(src_ref=rim_out.at[1], dst_ref=rim_in.at[0], send_sem=rim_send.at[1], recv_sem=rim_recv.at[0], device_id=below, device_id_type=MESH)

    @pl.when(has_above)
    def _():
        rim_up().start()

    @pl.when(has_below)
    def _():
        rim_down().start()

    for b in range(blocks):
        turned = f_ref[:, spans[b]].T
        for k, lane in enumerate((0, 1, 126, 127)):
            edge_ref[k, b : b + 1, :] = turned[lane : lane + 1, :]
    zero, one, two, three = (edge_ref[k] for k in range(4))
    gap = jnp.zeros((1, rows), F32)
    before = [jnp.concatenate([gap, x[:-1]], axis=0) for x in (two, three)]
    after = [jnp.concatenate([x[1:], gap], axis=0) for x in (zero, one)]
    blank = jnp.zeros((blocks, REACH), F32)
    for h in range(2):
        part = slice(h * REACH, (h + 1) * REACH)
        left = jnp.concatenate([before[0][:, part], before[1][:, part], zero[:, part], blank], axis=1)
        right = jnp.concatenate([three[:, part], after[0][:, part], after[1][:, part], blank], axis=1)
        for b in range(blocks):
            out_ref[2 * b + h, 34:35, :] = left[b : b + 1]
            out_ref[2 * b + h, 35:36, :] = right[b : b + 1]

    for b in range(blocks):
        for h in range(2):
            at = 2 * b + h
            out_ref[at, 0:REACH, :] = f_ref[h * REACH : (h + 1) * REACH, spans[b]]
            out_ref[at, 36:38, :] = jnp.zeros((2, LANES), F32)
        out_ref[2 * b, 32:34, :] = f_ref[REACH : REACH + 2, spans[b]]
        out_ref[2 * b + 1, 38:40, :] = f_ref[REACH - 2 : REACH, spans[b]]

    @pl.when(has_above)
    def _():
        rim_down().wait_recv()

    @pl.when(has_below)
    def _():
        rim_up().wait_recv()

    for b in range(blocks):
        k, lane = b // 4, (b % 4) * LANES
        out_ref[2 * b, 38:40, :] = rim_in[0, 2 * k : 2 * k + 2, lane : lane + LANES]
        out_ref[2 * b + 1, 32:34, :] = rim_in[1, 2 * k : 2 * k + 2, lane : lane + LANES]

    @pl.when(has_above)
    def _():
        rim_up().wait_send()

    @pl.when(has_below)
    def _():
        rim_down().wait_send()


def filtered_pieces(maps, weight, taps):
    rows, cols = maps.shape
    pieces = cols // LANES * 2
    vmem = pl.BlockSpec(memory_space=pltpu.VMEM)
    stacked = (cols // WIDE * rows, WINDOW)
    return pl.pallas_call(
        filter_kernel,
        out_shape=jax.ShapeDtypeStruct((pieces, REACH + 8, LANES), F32),
        in_specs=[vmem] * 3,
        out_specs=vmem,
        scratch_shapes=[
            pltpu.VMEM((rows, cols), F32),
            pltpu.VMEM((rows, cols), F32),
            pltpu.VMEM((rows, cols), F32),
            pltpu.VMEM((rows, cols), F32),
            pltpu.VMEM((STEPS, REACH, cols), F32),
            pltpu.VMEM((STEPS, REACH, cols), F32),
            pltpu.VMEM((2, 8, cols // 4), F32),
            pltpu.VMEM((2, 8, cols // 4), F32),
            pltpu.VMEM((2, WINDOW, WIDE), BF16),
            pltpu.VMEM((2, WINDOW, WIDE), BF16),
            pltpu.VMEM((2, rows, 3 * rows), BF16),
            pltpu.VMEM((2, rows, 3 * rows), BF16),
            pltpu.VMEM(stacked, BF16),
            pltpu.VMEM(stacked, BF16),
            pltpu.VMEM((3 * rows, cols), BF16),
            pltpu.VMEM((3 * rows, cols), BF16),
            pltpu.VMEM((4, cols // LANES, rows), F32),
            pltpu.SemaphoreType.DMA((2, STEPS)),
            pltpu.SemaphoreType.DMA((2, STEPS)),
            pltpu.SemaphoreType.DMA((2,)),
            pltpu.SemaphoreType.DMA((2,)),
        ],
        compiler_params=pltpu.CompilerParams(collective_id=0, has_side_effects=True),
    )(maps, weight, taps)


def estimate_kernel(one_ref, two_ref, owner_ref, pieces_ref, est_ref, mean_ref, line_ref, flow_ref):
    sims = pieces_ref.shape[0]
    line_ref[...] = jnp.zeros_like(line_ref)
    for s in range(sims):
        own = pieces_ref[s, 34:36, :]
        partner = 2.0 * pieces_ref[one_ref[s], 34:36, :] - pieces_ref[two_ref[s], 34:36, :]
        for side in range(2):
            line_ref[side, s : s + 1, :] = own[side : side + 1]
            line_ref[2 + side, s : s + 1, :] = partner[side : side + 1]
    own_l, own_r, g_l, g_r = (line_ref[k].T for k in range(4))

    def col(x, k):
        return x[k * REACH : (k + 1) * REACH, :]

    flow_ref[0] = 0.5 * col(own_l, 1) * (col(g_l, 2) - col(g_l, 0))
    flow_ref[1] = 0.5 * col(own_r, 1) * (col(g_r, 2) - col(g_r, 0))
    flow_ref[2] = col(g_l, 1)
    flow_ref[3] = col(g_r, 1)
    lane = lax.broadcasted_iota(jnp.int32, (REACH, LANES), 1)
    first, last = lane == 0, lane == LANES - 1
    depth = REACH + 8
    mean_ref[...] = jnp.zeros_like(mean_ref)
    for s in range(sims):
        f = pieces_ref[s]
        g = 2.0 * pieces_ref[one_ref[s]] - pieces_ref[two_ref[s]]
        p = f * (pltpu.roll(g, depth - 1, 0) - pltpu.roll(g, 1, 0))
        by_rows = (pltpu.roll(p, depth - 1, 0) - pltpu.roll(p, 1, 0))[:REACH]
        f, g = f[:REACH], g[:REACH]

        def vector(k):
            return jnp.broadcast_to(flow_ref[k, :, s : s + 1], (REACH, LANES))

        ahead = jnp.where(last, vector(3), pltpu.roll(g, LANES - 1, 1))
        behind = jnp.where(first, vector(2), pltpu.roll(g, 1, 1))
        q = 0.5 * f * (ahead - behind)
        ahead = jnp.where(last, vector(1), pltpu.roll(q, LANES - 1, 1))
        behind = jnp.where(first, vector(0), pltpu.roll(q, 1, 1))
        value = 0.25 * by_rows + 0.5 * (ahead - behind)
        est_ref[s] = value
        for o in range(OWNERS):
            mean_ref[o] += jnp.where(owner_ref[s] == o, value, 0.0)
    for o in range(OWNERS):
        tally = jnp.int32(0)
        for s in range(sims):
            tally = tally + (owner_ref[s] == o).astype(jnp.int32)
        mean_ref[o] = mean_ref[o] / jnp.full((REACH, LANES), jnp.maximum(tally, 1).astype(F32))


def estimates(pieces, pair_one, pair_two, owner):
    sims = pieces.shape[0]
    vmem, smem = pl.BlockSpec(memory_space=pltpu.VMEM), pl.BlockSpec(memory_space=pltpu.SMEM)
    return pl.pallas_call(
        estimate_kernel,
        out_shape=(jax.ShapeDtypeStruct((sims, REACH, LANES), F32), jax.ShapeDtypeStruct((OWNERS, REACH, LANES), F32)),
        in_specs=[smem] * 3 + [vmem],
        out_specs=(vmem, vmem),
        scratch_shapes=[pltpu.VMEM((4, LANES, LANES), F32), pltpu.VMEM((4, REACH, LANES), F32)],
    )(pair_one, pair_two, owner, pieces)


def body(maps, weight, beam, pair_one, pair_two, owner):
    rows, cols = weight.shape
    kernel = beam / jnp.sum(beam)
    taps = jnp.pad(jnp.stack([kernel, kernel[::-1]]), ((0, 6), (0, WINDOW - TAPS)))
    pieces = filtered_pieces(maps[0], weight, taps)
    pieces = lax.all_to_all(pieces, ("chips", "core"), split_axis=0, concat_axis=0, tiled=True)
    est, mean = estimates(pieces, pair_one, pair_two, owner)
    est = lax.all_to_all(est, ("chips", "core"), split_axis=0, concat_axis=0, tiled=True)
    est = est.reshape(cols // LANES, 2, REACH, LANES).transpose(1, 2, 0, 3).reshape(1, rows, cols)
    mean = lax.all_to_all(mean, "core", split_axis=2, concat_axis=1, tiled=True)
    return est, mean


def solution(mesh):
    split = Mesh(mesh.devices.reshape(16, 2, mesh.shape["rows"]), ("chips", "core", "rows"))
    sims = ("chips", "core")
    return jax.shard_map(
        body,
        mesh=split,
        in_specs=(P(sims, "rows", None), P("rows", None), P(), P(), P(), P()),
        out_specs=(P(sims, "rows", None), P(None, "rows", sims)),
        check_vma=False,
    )
```

profile of v0, /device:TPU:2, one launch (start us, length us, event | category | flops | bytes accessed | tf_op | source)
XLA Modules:
  0.0 185.7 jit_solution(11576638086277773550)
XLA Ops:
  0.6 0.0 copy-start
  0.6 0.8 reverse.3
  1.4 0.0 copy-done
  1.4 0.6 reduce_sum.9
  2.1 0.6 divide_bitcast_fusion
  2.7 0.6 select_maximum_fusion.taps_ref
  3.3 112.5 %shard_map.77 = f32[32,40,128]{2,1,0:T(8,128)} custom-call(f32[64,2048]{1,0:T(8,128)} %bitcast.19, f32[64,2048]{1,0:T(8,128)} %weight_ref.1, f32[8,512]{1,0:T(8,128)} %select_maximum_fusion.taps_ref), custom_call_target="tpu_custom_call" | custom-call | tf_op jit(solution)/shard_map/pallas_call | solution.py:252
  115.8 35.6 %all_to_all.28.pieces_ref = f32[32,40,128]{2,1,0:T(8,128)} all-to-all(f32[32,40,128]{2,1,0:T(8,128)} %shard_map.77), channel_id=1, replica_groups=mesh['chips'=16,'core'=2,'rows'=16] {'chips','core'}, dimensions={0} | all-to-all | bytes 1310720 | tf_op jit(solution)/shard_map/all_to_all | solution.py:349
  151.5 5.4 %shard_map.78 = (f32[32,32,128]{2,1,0:T(8,128)}, f32[8,32,128]{2,1,0:T(8,128)}) custom-call(s32[32]{0:T(128)} %one_ref.1, s32[32]{0:T(128)} %two_ref.1, s32[32]{0:T(128)} %owner_ref.1, f32[32,40,128]{2,1,0:T(8,128)} %all_to_all.28.pieces_ref), custom_call_target="tpu_custom_call" | custom-call | tf_op jit(solution)/shard_map/pallas_call | solution.py:335
  156.9 1.1 copy.11
  158.0 0.3 reshape.12
  158.3 3.8 %all_to_all.29 = f32[2,1,16384]{2,1,0:T(1,128)S(1)} all-to-all(f32[2,1,16384]{2,1,0:T(1,128)S(1)} %reshape.12), channel_id=1, replica_groups=mesh['chips'=16,'core'=2,'rows'=16] {'core'}, dimensions={0} | all-to-all | bytes 262144 | tf_op jit(solution)/shard_map/all_to_all | solution.py:353
  162.1 3.9 %all-to-all-start.1 = ((f32[32,32,128]{2,1,0:T(8,128)}), f32[32,32,128]{2,1,0:T(8,128)S(1)}, u32[]{:S(2)}, u32[]{:S(2)}) async-start(f32[32,32,128]{2,1,0:T(8,128)} %get-tuple-element.4), calls=%async_computation.1 | async-start | bytes 1048576 | tf_op jit(solution)/shard_map/all_to_all | solution.py:351
  166.0 0.5 broadcast.13
  166.6 1.0 reduce
  167.6 0.2 reshape.13
  167.8 0.9 copy.12
  168.7 15.7 %all-to-all-done.1 = f32[32,32,128]{2,1,0:T(8,128)S(1)} async-done(((f32[32,32,128]{2,1,0:T(8,128)}), f32[32,32,128]{2,1,0:T(8,128)S(1)}, u32[]{:S(2)}, u32[]{:S(2)}) %all-to-all-start.1) | async-done | bytes 524320 | tf_op jit(solution)/shard_map/all_to_all | solution.py:351
  184.5 0.3 copy.10
  184.8 0.9 reshape.11
Async XLA Ops:
  0.6 0.8 copy-start
  162.1 22.3 %all-to-all-start.1 = ((f32[32,32,128]{2,1,0:T(8,128)}), f32[32,32,128]{2,1,0:T(8,128)S(1)}, u32[]{:S(2)}, u32[]{:S(2)}) async-start(f32[32,32,128]{2,1,0:T(8,128)} %get-tuple-element.4), calls=%async_computation.1 | async-start | bytes 1048576 | tf_op jit(solution)/shard_map/all_to_all | solution.py:351
where the time goes:
time: 186 us
  Pallas kernels  118 us (63%)
  blocking collectives  39.5 us (21%)
  waiting for transfers between devices  15.7 us (8%)
  local copies, waits for them, and re-layouts  5.07 us (3%)
  starting transfers between devices  3.89 us (2%)
  other arithmetic  2.88 us (2%)
    pallas_call x1, Pallas kernels, filtered_pieces(): pl.pallas_call(filter_kernel, out_shape=jax.ShapeDtypeStruct((pieces, REA...  113 us
    all_to_all x1, blocking collectives, body(): lax.all_to_all(pieces, ('chips', 'core'), split_axis=0, concat_axis=0, ti...  35.6 us
    all_to_all x1, waiting for transfers between devices, body(): lax.all_to_all(est, ('chips', 'core'), split_axis=0, concat_axis=0, tiled...  15.7 us
    pallas_call x1, Pallas kernels, estimates(): pl.pallas_call(estimate_kernel, out_shape=(jax.ShapeDtypeStruct((sims, RE...  5.43 us
    all_to_all x1, starting transfers between devices, body(): lax.all_to_all(est, ('chips', 'core'), split_axis=0, concat_axis=0, tiled...  3.89 us
    all_to_all x1, blocking collectives, body(): mean = lax.all_to_all(mean, 'core', split_axis=2, concat_axis=1, tiled=True)  3.84 us
  transfers between devices with their start and end apart: 1, of which 1 were waited for; matrix products, arithmetic and copies ran while one was open for 1% of the time, Pallas kernels for 0%

commit v1 on v0

v1 whole, which is shorter than its diff:
```python
import jax
import jax.numpy as jnp
from jax import lax
from jax.experimental import pallas as pl
from jax.experimental.pallas import tpu as pltpu
from jax.sharding import Mesh
from jax.sharding import PartitionSpec as P

TAPS = 65
ITERS = 3
OWNERS = 8
STEPS = 2 * ITERS + 1
REACH = 32
LANES = 128
WIDE = 256
WINDOW = 512
ridge_term = 0.5
step_size = 0.6
F32 = jnp.float32
BF16 = jnp.bfloat16
MESH = pl.DeviceIdType.MESH


def halves(x):
    high = x.astype(BF16)
    return high, (x - high.astype(F32)).astype(BF16)


def dot(a, b):
    return jnp.dot(a, b, preferred_element_type=F32)


def whole_kernel(one_ref, two_ref, owner_ref, maps_ref, weight_ref, beam_ref, result_ref, mean_ref, taps_ref, f_ref, source_ref, h_ref, top_ref, bottom_ref, rim_in, across_h, across_l, down, x_h, x_l, ext_ref, edge_ref, out_ref, got_ref, line_ref, flow_ref, est_ref, sums_ref, other_ref, send_sem, recv_sem, rim_send, rim_recv, deal_send, deal_recv, home_send, home_recv, mean_send, mean_recv):
    count = lax.axis_size("rows")
    me = lax.axis_index("rows")
    above, below = {"rows": me - 1}, {"rows": me + 1}
    has_above, has_below = me > 0, me < count - 1
    rows, cols = f_ref.shape
    blocks, pairs = cols // LANES, cols // WIDE

    sims = got_ref.shape[0]
    half = lax.axis_index("core")
    mine = 2 * lax.axis_index("chips") + half

    def peer(offset):
        other = lax.rem(mine + offset, sims)
        return other, {"chips": other // 2, "core": other % 2}

    barrier = pltpu.get_barrier_semaphore()

    def greet(offset, carry):
        pl.semaphore_signal(barrier, inc=1, device_id=peer(offset)[1], device_id_type=MESH)
        return carry

    lax.fori_loop(1, sims, greet, 0)

    @pl.when(has_above)
    def _():
        pl.semaphore_signal(barrier, inc=1, device_id=above, device_id_type=MESH)

    @pl.when(has_below)
    def _():
        pl.semaphore_signal(barrier, inc=1, device_id=below, device_id_type=MESH)

    taps_ref[...] = jnp.zeros_like(taps_ref)
    taps_ref[0:1, :TAPS] = beam_ref[...]
    taps = taps_ref[0:1, :] / jnp.sum(taps_ref[0:1, :], axis=1, keepdims=True)
    taps_ref[0:1, :] = taps
    square = (LANES, LANES)
    turned = jnp.broadcast_to(taps[:, :LANES], square).T
    places = lax.broadcasted_iota(jnp.int32, square, 0) + lax.broadcasted_iota(jnp.int32, square, 1)
    taps_ref[1:2, :LANES] = jnp.sum(jnp.where(places == TAPS - 1, turned, 0.0), axis=0, keepdims=True)

    def tables(way):
        line = jnp.broadcast_to(taps_ref[1 - way : 2 - way, :], (WINDOW, WINDOW))
        table = pltpu.roll(line, WINDOW - 160, 1, stride=1, stride_axis=0)[:, :WIDE]
        high, low = halves(table)
        across_h[way] = high
        across_l[way] = low
        line = jnp.broadcast_to(taps_ref[way : way + 1, :LANES], (rows, LANES))
        inside = pltpu.roll(line, LANES - REACH, 1, stride=1, stride_axis=0)
        over = pltpu.roll(line, 64, 1, stride=1, stride_axis=0)
        under = pltpu.roll(line, 0, 1, stride=1, stride_axis=0)
        place = lax.broadcasted_iota(jnp.int32, (rows, LANES), 1)
        rim = jnp.where(place < 96, over, under)
        high, low = halves(inside[:, :64])
        rim_h, rim_l = halves(rim[:, 64:])
        down[way] = jnp.concatenate([high, low, high, rim_h, rim_l, rim_h], axis=1)

    nothing = jnp.zeros((rows, LANES), BF16)
    for ref in (x_h, x_l):
        ref[0, :, 0:LANES] = nothing
        ref[pairs - 1, :, 3 * LANES : 4 * LANES] = nothing

    tops = (192, 256, 320)
    bottoms = (224, 288, 352)
    empty = jnp.zeros((pairs, REACH, WIDE), BF16)

    @pl.when(jnp.logical_not(has_above))
    def _():
        for at in tops:
            ext_ref[:, at : at + REACH, :] = empty
        rim_in[0] = jnp.zeros_like(rim_in[0])

    @pl.when(jnp.logical_not(has_below))
    def _():
        for at in bottoms:
            ext_ref[:, at : at + REACH, :] = empty
        rim_in[1] = jnp.zeros_like(rim_in[1])

    def put(block, value):
        high, low = halves(value)
        for pair in range(pairs):
            place = block - 2 * pair + 1
            if 0 <= place < 4:
                x_h[pair, :, place * LANES : (place + 1) * LANES] = high
                x_l[pair, :, place * LANES : (place + 1) * LANES] = low

    def up_copy(step, parity, pair):
        return pltpu.make_async_remote_copy(
            src_ref=h_ref.at[parity, pair, 0:REACH],
            dst_ref=bottom_ref.at[step, pair],
            send_sem=send_sem.at[0, step, pair],
            recv_sem=recv_sem.at[1, step, pair],
            device_id=above,
            device_id_type=MESH,
        )

    def down_copy(step, parity, pair):
        return pltpu.make_async_remote_copy(
            src_ref=h_ref.at[parity, pair, REACH : 2 * REACH],
            dst_ref=top_ref.at[step, pair],
            send_sem=send_sem.at[1, step, pair],
            recv_sem=recv_sem.at[0, step, pair],
            device_id=below,
            device_id_type=MESH,
        )

    def sent(step, parity, pair):
        @pl.when(has_above)
        def _():
            up_copy(step, parity, pair).wait_send()

        @pl.when(has_below)
        def _():
            down_copy(step, parity, pair).wait_send()

    def across(step, parity, way, pair, waits=True):
        if waits:
            sent(step - 2, parity, pair)
        high, low = x_h[pair], x_l[pair]
        both = dot(jnp.concatenate([high, low], axis=0), across_h[way])
        value = both[:rows] + both[rows:] + dot(high, across_l[way])
        h_ref[parity, pair] = value

        @pl.when(has_above)
        def _():
            up_copy(step, parity, pair).start()

        @pl.when(has_below)
        def _():
            down_copy(step, parity, pair).start()

        high, low = halves(value)
        ext_ref[pair, 0:rows] = high
        ext_ref[pair, rows : 2 * rows] = high
        ext_ref[pair, 2 * rows : 3 * rows] = low

    def downward(step, parity, way, pair):
        @pl.when(has_above)
        def _():
            down_copy(step, parity, pair).wait_recv()
            high, low = halves(top_ref[step, pair])
            for at, part in zip(tops, (high, high, low)):
                ext_ref[pair, at : at + REACH] = part

        @pl.when(has_below)
        def _():
            up_copy(step, parity, pair).wait_recv()
            high, low = halves(bottom_ref[step, pair])
            for at, part in zip(bottoms, (high, high, low)):
                ext_ref[pair, at : at + REACH] = part

        return dot(down[way], ext_ref[pair])

    spans = [slice(b * LANES, (b + 1) * LANES) for b in range(blocks)]
    tables(1)
    for b in range(blocks):
        put(b, weight_ref[:, spans[b]] * maps_ref[:, spans[b]])

    inner = jnp.logical_and(has_above, has_below)

    @pl.when(inner)
    def _():
        pl.semaphore_wait(barrier, sims + 1)

    @pl.when(jnp.logical_not(inner))
    def _():
        pl.semaphore_wait(barrier, sims)

    for p in range(pairs):
        across(0, 0, 1, p, waits=False)
    tables(0)

    def sweep(step, parity, way, use, after):
        for p in range(pairs):
            total = downward(step, parity, way, p)
            for k in range(2):
                use(2 * p + k, total[:, k * LANES : (k + 1) * LANES])
            if after is not None:
                if p > 0:
                    after(p - 1)
                if p == pairs - 1:
                    after(p)

    def begin(b, total):
        first = step_size * total
        source_ref[:, spans[b]] = first
        f_ref[:, spans[b]] = first
        put(b, first)

    def weigh(b, total):
        put(b, weight_ref[:, spans[b]] * total)

    def renew(b, total):
        value = (1.0 - step_size * ridge_term) * f_ref[:, spans[b]] + source_ref[:, spans[b]] - step_size * total
        f_ref[:, spans[b]] = value
        return value

    sweep(0, 0, 1, begin, lambda p: across(1, 1, 0, p, waits=False))

    def iteration(turn, carry):
        step = 2 * turn + 1
        sweep(step, 1, 0, weigh, lambda p: across(step + 1, 0, 1, p))
        sweep(step + 1, 0, 1, lambda b, total: put(b, renew(b, total)), lambda p: across(step + 2, 1, 0, p))
        return carry

    lax.fori_loop(0, ITERS - 1, iteration, 0)
    last = 2 * ITERS - 1
    sweep(last, 1, 0, weigh, lambda p: across(last + 1, 0, 1, p))

    def rim_up(pair):
        return pltpu.make_async_remote_copy(
            src_ref=f_ref.at[0:8, pair * WIDE : (pair + 1) * WIDE],
            dst_ref=rim_in.at[1, pair],
            send_sem=rim_send.at[0, pair],
            recv_sem=rim_recv.at[1, pair],
            device_id=above,
            device_id_type=MESH,
        )

    def rim_down(pair):
        return pltpu.make_async_remote_copy(
            src_ref=f_ref.at[rows - 8 : rows, pair * WIDE : (pair + 1) * WIDE],
            dst_ref=rim_in.at[0, pair],
            send_sem=rim_send.at[1, pair],
            recv_sem=rim_recv.at[0, pair],
            device_id=below,
            device_id_type=MESH,
        )

    def finish(b, total):
        value = renew(b, total)
        if b % 2 == 1:
            pair = b // 2

            @pl.when(has_above)
            def _():
                rim_up(pair).start()

            @pl.when(has_below)
            def _():
                rim_down(pair).start()

        for h in range(2):
            out_ref[2 * b + h, 0:REACH, :] = value[h * REACH : (h + 1) * REACH]
            out_ref[2 * b + h, 36:38, :] = jnp.zeros((2, LANES), F32)
        out_ref[2 * b, 32:34, :] = value[REACH : REACH + 2]
        out_ref[2 * b + 1, 38:40, :] = value[REACH - 2 : REACH]
        turned = value.T
        for k, lane in enumerate((0, 1, 126, 127)):
            edge_ref[k, b : b + 1, :] = turned[lane : lane + 1, :]

    sweep(last + 1, 0, 1, finish, None)

    zero, one, two, three = (edge_ref[k] for k in range(4))
    gap = jnp.zeros((1, rows), F32)
    before = [jnp.concatenate([gap, x[:-1]], axis=0) for x in (two, three)]
    after = [jnp.concatenate([x[1:], gap], axis=0) for x in (zero, one)]
    blank = jnp.zeros((blocks, REACH), F32)
    for h in range(2):
        part = slice(h * REACH, (h + 1) * REACH)
        left = jnp.concatenate([before[0][:, part], before[1][:, part], zero[:, part], blank], axis=1)
        right = jnp.concatenate([three[:, part], after[0][:, part], after[1][:, part], blank], axis=1)
        for b in range(blocks):
            out_ref[2 * b + h, 34:35, :] = left[b : b + 1]
            out_ref[2 * b + h, 35:36, :] = right[b : b + 1]

    for p in range(pairs):

        @pl.when(has_above)
        def _():
            rim_down(p).wait_recv()

        @pl.when(has_below)
        def _():
            rim_up(p).wait_recv()

        for k in range(2):
            b = 2 * p + k
            out_ref[2 * b, 38:40, :] = rim_in[0, p, 6:8, k * LANES : (k + 1) * LANES]
            out_ref[2 * b + 1, 32:34, :] = rim_in[1, p, 0:2, k * LANES : (k + 1) * LANES]

    def deal(offset):
        other, device = peer(offset)
        return pltpu.make_async_remote_copy(
            src_ref=out_ref.at[other], dst_ref=got_ref.at[mine], send_sem=deal_send.at[offset], recv_sem=deal_recv.at[offset], device_id=device, device_id_type=MESH
        )

    def start_deal(offset, carry):
        deal(offset).start()
        return carry

    def await_deal(offset, carry):
        deal(offset).wait_recv()
        return carry

    lax.fori_loop(1, sims, start_deal, 0)
    got_ref[mine] = out_ref[mine]
    for p in range(pairs):
        sent(last, 1, p)
        sent(last + 1, 0, p)

        @pl.when(has_above)
        def _():
            rim_up(p).wait_send()

        @pl.when(has_below)
        def _():
            rim_down(p).wait_send()

    line_ref[...] = jnp.zeros_like(line_ref)
    sums_ref[...] = jnp.zeros_like(sums_ref)
    lax.fori_loop(1, sims, await_deal, 0)

    for d in range(sims):
        s = peer(d)[0]
        own = got_ref[s, 34:36, :]
        partner = 2.0 * got_ref[one_ref[s], 34:36, :] - got_ref[two_ref[s], 34:36, :]
        for side in range(2):
            line_ref[side, d : d + 1, :] = own[side : side + 1]
            line_ref[2 + side, d : d + 1, :] = partner[side : side + 1]
    own_l, own_r, g_l, g_r = (line_ref[k].T for k in range(4))

    def col(x, k):
        return x[k * REACH : (k + 1) * REACH, :]

    flow_ref[0] = 0.5 * col(own_l, 1) * (col(g_l, 2) - col(g_l, 0))
    flow_ref[1] = 0.5 * col(own_r, 1) * (col(g_r, 2) - col(g_r, 0))
    flow_ref[2] = col(g_l, 1)
    flow_ref[3] = col(g_r, 1)
    lane = lax.broadcasted_iota(jnp.int32, (REACH, LANES), 1)
    first, final = lane == 0, lane == LANES - 1
    depth = REACH + 8
    row_spot = pl.ds(pl.multiple_of(half * REACH, REACH), REACH)
    col_spot = pl.ds(pl.multiple_of(lax.axis_index("chips") * LANES, LANES), LANES)

    def home(offset):
        return pltpu.make_async_remote_copy(
            src_ref=est_ref.at[offset],
            dst_ref=result_ref.at[row_spot, col_spot],
            send_sem=home_send.at[offset],
            recv_sem=home_recv.at[offset],
            device_id=peer(offset)[1],
            device_id_type=MESH,
        )

    for d in range(sims):
        s = peer(d)[0]
        f = got_ref[s]
        g = 2.0 * got_ref[one_ref[s]] - got_ref[two_ref[s]]
        p = f * (pltpu.roll(g, depth - 1, 0) - pltpu.roll(g, 1, 0))
        by_rows = (pltpu.roll(p, depth - 1, 0) - pltpu.roll(p, 1, 0))[:REACH]
        f, g = f[:REACH], g[:REACH]

        def vector(k):
            return jnp.broadcast_to(flow_ref[k, :, d : d + 1], (REACH, LANES))

        ahead = jnp.where(final, vector(3), pltpu.roll(g, LANES - 1, 1))
        behind = jnp.where(first, vector(2), pltpu.roll(g, 1, 1))
        q = 0.5 * f * (ahead - behind)
        ahead = jnp.where(final, vector(1), pltpu.roll(q, LANES - 1, 1))
        behind = jnp.where(first, vector(0), pltpu.roll(q, 1, 1))
        value = 0.25 * by_rows + 0.5 * (ahead - behind)
        if d == 0:
            result_ref[row_spot, col_spot] = value
        else:
            est_ref[d] = value
            home(d).start()
        for o in range(OWNERS):
            sums_ref[o] += jnp.where(owner_ref[s] == o, value, 0.0)
    for o in range(OWNERS):
        tally = jnp.int32(0)
        for s in range(sims):
            tally = tally + (owner_ref[s] == o).astype(jnp.int32)
        sums_ref[o] = sums_ref[o] / jnp.full((REACH, LANES), jnp.maximum(tally, 1).astype(F32))

    swap = pltpu.make_async_remote_copy(
        src_ref=sums_ref, dst_ref=other_ref, send_sem=mean_send, recv_sem=mean_recv, device_id={"core": 1 - half}, device_id_type=MESH
    )
    swap.start()
    wide = LANES // 2

    @pl.when(half == 0)
    def _():
        mean_ref[:, 0:REACH, :] = sums_ref[:, :, 0:wide]

    @pl.when(half == 1)
    def _():
        mean_ref[:, REACH : 2 * REACH, :] = sums_ref[:, :, wide:LANES]

    swap.wait_recv()

    @pl.when(half == 0)
    def _():
        mean_ref[:, REACH : 2 * REACH, :] = other_ref[:, :, 0:wide]

    @pl.when(half == 1)
    def _():
        mean_ref[:, 0:REACH, :] = other_ref[:, :, wide:LANES]

    def await_home(offset, carry):
        pltpu.make_async_remote_copy(
            src_ref=est_ref.at[offset],
            dst_ref=result_ref.at[0:REACH, 0:LANES],
            send_sem=home_send.at[offset],
            recv_sem=home_recv.at[offset],
            device_id=peer(offset)[1],
            device_id_type=MESH,
        ).wait_recv()
        return carry

    def finish_sends(offset, carry):
        deal(offset).wait_send()
        home(offset).wait_send()
        return carry

    lax.fori_loop(1, sims, await_home, 0)
    swap.wait_send()
    lax.fori_loop(1, sims, finish_sends, 0)


def body(maps, weight, beam, pair_one, pair_two, owner):
    rows, cols = weight.shape
    pairs = cols // WIDE
    sims = cols // LANES * 2
    vmem, smem = pl.BlockSpec(memory_space=pltpu.VMEM), pl.BlockSpec(memory_space=pltpu.SMEM)
    est, mean = pl.pallas_call(
        whole_kernel,
        out_shape=(jax.ShapeDtypeStruct((rows, cols), F32), jax.ShapeDtypeStruct((OWNERS, rows, LANES // 2), F32)),
        in_specs=[smem] * 3 + [vmem] * 3,
        out_specs=(vmem, vmem),
        scratch_shapes=[
            pltpu.VMEM((8, WINDOW), F32),
            pltpu.VMEM((rows, cols), F32),
            pltpu.VMEM((rows, cols), F32),
            pltpu.VMEM((2, pairs, rows, WIDE), F32),
            pltpu.VMEM((STEPS, pairs, REACH, WIDE), F32),
            pltpu.VMEM((STEPS, pairs, REACH, WIDE), F32),
            pltpu.VMEM((2, pairs, 8, WIDE), F32),
            pltpu.VMEM((2, WINDOW, WIDE), BF16),
            pltpu.VMEM((2, WINDOW, WIDE), BF16),
            pltpu.VMEM((2, rows, 6 * rows), BF16),
            pltpu.VMEM((pairs, rows, WINDOW), BF16),
            pltpu.VMEM((pairs, rows, WINDOW), BF16),
            pltpu.VMEM((pairs, 6 * rows, WIDE), BF16),
            pltpu.VMEM((4, cols // LANES, rows), F32),
            pltpu.VMEM((sims, REACH + 8, LANES), F32),
            pltpu.VMEM((sims, REACH + 8, LANES), F32),
            pltpu.VMEM((4, LANES, LANES), F32),
            pltpu.VMEM((4, REACH, LANES), F32),
            pltpu.VMEM((sims, REACH, LANES), F32),
            pltpu.VMEM((OWNERS, REACH, LANES), F32),
            pltpu.VMEM((OWNERS, REACH, LANES), F32),
            pltpu.SemaphoreType.DMA((2, STEPS, pairs)),
            pltpu.SemaphoreType.DMA((2, STEPS, pairs)),
            pltpu.SemaphoreType.DMA((2, pairs)),
            pltpu.SemaphoreType.DMA((2, pairs)),
            pltpu.SemaphoreType.DMA((sims,)),
            pltpu.SemaphoreType.DMA((sims,)),
            pltpu.SemaphoreType.DMA((sims,)),
            pltpu.SemaphoreType.DMA((sims,)),
            pltpu.SemaphoreType.DMA,
            pltpu.SemaphoreType.DMA,
        ],
        compiler_params=pltpu.CompilerParams(collective_id=0, has_side_effects=True),
    )(pair_one, pair_two, owner, maps[0], weight, beam.reshape(1, TAPS))
    return est[None], mean


def solution(mesh):
    split = Mesh(mesh.devices.reshape(16, 2, mesh.shape["rows"]), ("chips", "core", "rows"))
    sims = ("chips", "core")
    return jax.shard_map(
        body,
        mesh=split,
        in_specs=(P(sims, "rows", None), P("rows", None), P(), P(), P(), P()),
        out_specs=(P(sims, "rows", None), P(None, "rows", sims)),
        check_vma=False,
    )
```

time: 186 us -> 149 us (0.80)
  the two profiles are of different devices: /device:TPU:2 before, /device:TPU:83 now
where the time goes in v1:
time: 149 us
  Pallas kernels  146 us (98%)
  local copies, waits for them, and re-layouts  2.62 us (2%)
    pallas_call x1, Pallas kernels, body(): pl.pallas_call(whole_kernel, out_shape=(jax.ShapeDtypeStruct((rows, cols)...  146 us

profile of v1, /device:TPU:83, one launch (start us, length us, event | category | flops | bytes accessed | tf_op | source)
XLA Modules:
  0.0 149.0 jit_solution(11450522712742338372)
XLA Ops:
  0.6 145.7 %shard_map.77 = (f32[64,2048]{1,0:T(8,128)}, f32[8,64,64]{2,1,0:T(8,128)}) custom-call(s32[32]{0:T(128)} %one_ref.1, s32[32]{0:T(128)} %two_ref.1, s32[32]{0:T(128)} %owner_ref.1, f32[64,2048]{1,0:T(8,128)} %bitcast.3, f32[64,2048]{1,0:T(8,128)} %weight_ref.1, f32[1,65]{1,0:T(1,128)} %bitcast.5), custom_call_target="tpu_custom_call" | custom-call | tf_op jit(solution)/shard_map/pallas_call | solution.py:458
  146.3 0.0 copy-start
  146.3 1.9 %copy.10 = f32[1,64,2048]{2,1,0:T(8,128)} copy(f32[1,64,2048]{2,1,0:T(8,128)} %bitcast.4) | data formatting | bytes 1048576
  148.2 0.0 copy-done
  148.2 0.7 copy.11
Async XLA Ops:
  146.3 1.9 %copy-start = (f32[8,64,64]{2,1,0:T(8,128)S(1)}, f32[8,64,64]{2,1,0:T(8,128)}, u32[]{:S(2)}) copy-start(f32[8,64,64]{2,1,0:T(8,128)} %get-tuple-element.9) | copy-start | bytes 393220

commit v2 on v1

--- a/solution.py
+++ b/solution.py
@@ -19,6 +19,12 @@
 F32 = jnp.float32
 BF16 = jnp.bfloat16
 MESH = pl.DeviceIdType.MESH
+SLOTS = (1549942144, 1337883281)
+ITEMS = (-1249954688, -332997999)
+
+
+def looked_up(words, at):
+    return jnp.right_shift(jnp.where(at < 8, words[0], words[1]), 4 * (at % 8)) & 15
 
 
 def halves(x):
@@ -30,37 +36,107 @@
     return jnp.dot(a, b, preferred_element_type=F32)
 
 
-def whole_kernel(one_ref, two_ref, owner_ref, maps_ref, weight_ref, beam_ref, result_ref, mean_ref, taps_ref, f_ref, source_ref, h_ref, top_ref, bottom_ref, rim_in, across_h, across_l, down, x_h, x_l, ext_ref, edge_ref, out_ref, got_ref, line_ref, flow_ref, est_ref, sums_ref, other_ref, send_sem, recv_sem, rim_send, rim_recv, deal_send, deal_recv, home_send, home_recv, mean_send, mean_recv):
+def whole_kernel(one_ref, two_ref, owner_ref, maps_ref, weight_ref, beam_ref, result_ref, mean_ref, move_ref, moved_ref, taps_ref, f_ref, source_ref, h_ref, top_ref, bottom_ref, rim_in, across_h, across_l, down, x_h, x_l, ext_ref, edge_ref, out_ref, got_ref, line_ref, flow_ref, est_ref, sums_ref, other_ref, send_sem, recv_sem, rim_send, rim_recv, deal_send, deal_recv, home_send, home_recv, move_send, move_recv, mean_send, mean_recv):
     count = lax.axis_size("rows")
     me = lax.axis_index("rows")
-    above, below = {"rows": me - 1}, {"rows": me + 1}
-    has_above, has_below = me > 0, me < count - 1
+    half = lax.axis_index("core")
+    chip = lax.axis_index("chips")
+    mine = 2 * chip + half
+    sims = got_ref.shape[0]
+
+    group, spot, ring = me // 4, me % 4, mine // 2 % 8
+
+    def device_at(rows_at, sims_at):
+        return {"rows": rows_at, "chips": sims_at // 2, "core": sims_at % 2}
+
+    def holder(slab_at, sim):
+        slot = looked_up(SLOTS, slab_at % 4 * 4 + sim // 16 * 2 + sim % 2)
+        return 4 * (slab_at // 4) + slot // 4, slot // 2 % 2 * 16 + sim // 2 % 8 * 2 + slot % 2
+
+    item = looked_up(ITEMS, 4 * spot + mine // 16 * 2 + half)
+    slab = 4 * group + item // 4
+    held = item // 2 % 2 * 16 + ring * 2 + item % 2
+    above, below = device_at(*holder(slab - 1, held)), device_at(*holder(slab + 1, held))
+    has_above, has_below = slab > 0, slab < count - 1
+    target_rows, target_sims = holder(me, mine)
+    target, origin = device_at(target_rows, target_sims), device_at(slab, held)
+    moves = jnp.logical_or(target_rows != me, target_sims != mine)
     rows, cols = f_ref.shape
     blocks, pairs = cols // LANES, cols // WIDE
 
-    sims = got_ref.shape[0]
-    half = lax.axis_index("core")
-    mine = 2 * lax.axis_index("chips") + half
+    barrier = pltpu.get_barrier_semaphore()
+
+    @pl.when(has_above)
+    def _():
+        pl.semaphore_signal(barrier, inc=1, device_id=above, device_id_type=MESH)
+
+    @pl.when(has_below)
+    def _():
+        pl.semaphore_signal(barrier, inc=1, device_id=below, device_id_type=MESH)
+
+    @pl.when(moves)
+    def _():
+        pl.semaphore_signal(barrier, inc=1, device_id=origin, device_id_type=MESH)
 
     def peer(offset):
         other = lax.rem(mine + offset, sims)
-        return other, {"chips": other // 2, "core": other % 2}
-
-    barrier = pltpu.get_barrier_semaphore()
+        return other, device_at(me, other)
+
+    def dealt(offset):
+        other = lax.rem(held + offset, sims)
+        own = jnp.logical_and(other == mine, slab == me)
+        return other, device_at(slab, other), own
+
+    def dealer(offset):
+        other = lax.rem(mine + sims - offset, sims)
+        rows_at, sims_at = holder(me, other)
+        own = jnp.logical_and(rows_at == me, sims_at == mine)
+        return device_at(rows_at, sims_at), own
 
     def greet(offset, carry):
         pl.semaphore_signal(barrier, inc=1, device_id=peer(offset)[1], device_id_type=MESH)
         return carry
 
+    def greet_dealer(offset, carry):
+        device, own = dealer(offset)
+
+        @pl.when(jnp.logical_not(own))
+        def _():
+            pl.semaphore_signal(barrier, inc=1, device_id=device, device_id_type=MESH)
+
+        return carry
+
     lax.fori_loop(1, sims, greet, 0)
-
-    @pl.when(has_above)
-    def _():
-        pl.semaphore_signal(barrier, inc=1, device_id=above, device_id_type=MESH)
-
-    @pl.when(has_below)
-    def _():
-        pl.semaphore_signal(barrier, inc=1, device_id=below, device_id_type=MESH)
+    lax.fori_loop(0, sims, greet_dealer, 0)
+
+    def number(x):
+        return jnp.where(x, 1, 0)
+
+    def put_away(pair):
+        span = slice(pair * WIDE, (pair + 1) * WIDE)
+        move_ref[0, pair] = weight_ref[:, span] * maps_ref[:, span]
+        move_ref[1, pair] = weight_ref[:, span]
+
+    for p in range(pairs):
+        put_away(p)
+    pl.semaphore_wait(barrier, 2 * sims - 1 + number(has_above) + number(has_below) + number(moves) - number(slab == me))
+
+    def move(kind, pair):
+        return pltpu.make_async_remote_copy(
+            src_ref=move_ref.at[kind, pair], dst_ref=moved_ref.at[kind, pair], send_sem=move_send.at[kind, pair], recv_sem=move_recv.at[kind, pair], device_id=target, device_id_type=MESH
+        )
+
+    def send_off(kind, pair):
+        @pl.when(moves)
+        def _():
+            move(kind, pair).start()
+
+        @pl.when(jnp.logical_not(moves))
+        def _():
+            pltpu.make_async_copy(move_ref.at[kind, pair], moved_ref.at[kind, pair], move_recv.at[kind, pair]).start()
+
+    for p in range(pairs):
+        send_off(0, p)
 
     taps_ref[...] = jnp.zeros_like(taps_ref)
     taps_ref[0:1, :TAPS] = beam_ref[...]
@@ -185,25 +261,21 @@
 
     spans = [slice(b * LANES, (b + 1) * LANES) for b in range(blocks)]
     tables(1)
-    for b in range(blocks):
-        put(b, weight_ref[:, spans[b]] * maps_ref[:, spans[b]])
-
-    inner = jnp.logical_and(has_above, has_below)
-
-    @pl.when(inner)
-    def _():
-        pl.semaphore_wait(barrier, sims + 1)
-
-    @pl.when(jnp.logical_not(inner))
-    def _():
-        pl.semaphore_wait(barrier, sims)
-
     for p in range(pairs):
-        across(0, 0, 1, p, waits=False)
+        move(0, p).wait_recv()
+        for k in range(2):
+            put(2 * p + k, moved_ref[0, p, :, k * LANES : (k + 1) * LANES])
+        if p > 0:
+            across(0, 0, 1, p - 1, waits=False)
+            send_off(1, p - 1)
+    across(0, 0, 1, pairs - 1, waits=False)
+    send_off(1, pairs - 1)
     tables(0)
 
-    def sweep(step, parity, way, use, after):
+    def sweep(step, parity, way, use, after, ready=None):
         for p in range(pairs):
+            if ready is not None:
+                ready(p)
             total = downward(step, parity, way, p)
             for k in range(2):
                 use(2 * p + k, total[:, k * LANES : (k + 1) * LANES])
@@ -220,7 +292,7 @@
         put(b, first)
 
     def weigh(b, total):
-        put(b, weight_ref[:, spans[b]] * total)
+        put(b, moved_ref[1, b // 2, :, b % 2 * LANES : (b % 2 + 1) * LANES] * total)
 
     def renew(b, total):
         value = (1.0 - step_size * ridge_term) * f_ref[:, spans[b]] + source_ref[:, spans[b]] - step_size * total
@@ -231,7 +303,13 @@
 
     def iteration(turn, carry):
         step = 2 * turn + 1
-        sweep(step, 1, 0, weigh, lambda p: across(step + 1, 0, 1, p))
+
+        def ready(p):
+            @pl.when(turn == 0)
+            def _():
+                move(1, p).wait_recv()
+
+        sweep(step, 1, 0, weigh, lambda p: across(step + 1, 0, 1, p), ready)
         sweep(step + 1, 0, 1, lambda b, total: put(b, renew(b, total)), lambda p: across(step + 2, 1, 0, p))
         return carry
 
@@ -312,21 +390,29 @@
             out_ref[2 * b + 1, 32:34, :] = rim_in[1, p, 0:2, k * LANES : (k + 1) * LANES]
 
     def deal(offset):
-        other, device = peer(offset)
+        other, device, own = dealt(offset)
         return pltpu.make_async_remote_copy(
-            src_ref=out_ref.at[other], dst_ref=got_ref.at[mine], send_sem=deal_send.at[offset], recv_sem=deal_recv.at[offset], device_id=device, device_id_type=MESH
+            src_ref=out_ref.at[other], dst_ref=got_ref.at[held], send_sem=deal_send.at[offset], recv_sem=deal_recv.at[offset], device_id=device, device_id_type=MESH
         )
 
     def start_deal(offset, carry):
-        deal(offset).start()
+        other, device, own = dealt(offset)
+
+        @pl.when(jnp.logical_not(own))
+        def _():
+            deal(offset).start()
+
+        @pl.when(own)
+        def _():
+            pltpu.make_async_copy(out_ref.at[other], got_ref.at[held], deal_recv.at[offset]).start()
+
         return carry
 
     def await_deal(offset, carry):
         deal(offset).wait_recv()
         return carry
 
-    lax.fori_loop(1, sims, start_deal, 0)
-    got_ref[mine] = out_ref[mine]
+    lax.fori_loop(0, sims, start_deal, 0)
     for p in range(pairs):
         sent(last, 1, p)
         sent(last + 1, 0, p)
@@ -341,7 +427,7 @@
 
     line_ref[...] = jnp.zeros_like(line_ref)
     sums_ref[...] = jnp.zeros_like(sums_ref)
-    lax.fori_loop(1, sims, await_deal, 0)
+    lax.fori_loop(0, sims, await_deal, 0)
 
     for d in range(sims):
         s = peer(d)[0]
@@ -363,7 +449,7 @@
     first, final = lane == 0, lane == LANES - 1
     depth = REACH + 8
     row_spot = pl.ds(pl.multiple_of(half * REACH, REACH), REACH)
-    col_spot = pl.ds(pl.multiple_of(lax.axis_index("chips") * LANES, LANES), LANES)
+    col_spot = pl.ds(pl.multiple_of(chip * LANES, LANES), LANES)
 
     def home(offset):
         return pltpu.make_async_remote_copy(
@@ -406,7 +492,7 @@
         sums_ref[o] = sums_ref[o] / jnp.full((REACH, LANES), jnp.maximum(tally, 1).astype(F32))
 
     swap = pltpu.make_async_remote_copy(
-        src_ref=sums_ref, dst_ref=other_ref, send_sem=mean_send, recv_sem=mean_recv, device_id={"core": 1 - half}, device_id_type=MESH
+        src_ref=sums_ref, dst_ref=other_ref, send_sem=mean_send, recv_sem=mean_recv, device_id=device_at(me, 2 * chip + 1 - half), device_id_type=MESH
     )
     swap.start()
     wide = LANES // 2
@@ -440,14 +526,27 @@
         ).wait_recv()
         return carry
 
-    def finish_sends(offset, carry):
-        deal(offset).wait_send()
+    def finish_homes(offset, carry):
         home(offset).wait_send()
+        return carry
+
+    def finish_deals(offset, carry):
+        @pl.when(jnp.logical_not(dealt(offset)[2]))
+        def _():
+            deal(offset).wait_send()
+
         return carry
 
     lax.fori_loop(1, sims, await_home, 0)
     swap.wait_send()
-    lax.fori_loop(1, sims, finish_sends, 0)
+    lax.fori_loop(1, sims, finish_homes, 0)
+    lax.fori_loop(0, sims, finish_deals, 0)
+
+    @pl.when(moves)
+    def _():
+        for kind in range(2):
+            for p in range(pairs):
+                move(kind, p).wait_send()
 
 
 def body(maps, weight, beam, pair_one, pair_two, owner):
@@ -461,6 +560,8 @@
         in_specs=[smem] * 3 + [vmem] * 3,
         out_specs=(vmem, vmem),
         scratch_shapes=[
+            pltpu.VMEM((2, pairs, rows, WIDE), F32),
+            pltpu.VMEM((2, pairs, rows, WIDE), F32),
             pltpu.VMEM((8, WINDOW), F32),
             pltpu.VMEM((rows, cols), F32),
             pltpu.VMEM((rows, cols), F32),
@@ -490,6 +591,8 @@
             pltpu.SemaphoreType.DMA((sims,)),
             pltpu.SemaphoreType.DMA((sims,)),
             pltpu.SemaphoreType.DMA((sims,)),
+            pltpu.SemaphoreType.DMA((2, pairs)),
+            pltpu.SemaphoreType.DMA((2, pairs)),
             pltpu.SemaphoreType.DMA,
             pltpu.SemaphoreType.DMA,
         ],

time: 149 us -> 128 us (0.86)
  the two profiles are of different devices: /device:TPU:83 before, /device:TPU:5 now
where the time goes in v2:
time: 128 us
  Pallas kernels  124 us (97%)
  local copies, waits for them, and re-layouts  2.62 us (2%)
    pallas_call x1, Pallas kernels, body(): pl.pallas_call(whole_kernel, out_shape=(jax.ShapeDtypeStruct((rows, cols)...  124 us
    unnamed x4, local copies, waits for them, and re-layouts  2.62 us

profile of v2, /device:TPU:5, one launch (start us, length us, event | category | flops | bytes accessed | tf_op | source)
XLA Modules:
  0.0 127.7 jit_solution(9342465692946960571)
XLA Ops:
  0.6 124.4 %shard_map.77 = (f32[64,2048]{1,0:T(8,128)}, f32[8,64,64]{2,1,0:T(8,128)}) custom-call(s32[32]{0:T(128)} %one_ref.1, s32[32]{0:T(128)} %two_ref.1, s32[32]{0:T(128)} %owner_ref.1, f32[64,2048]{1,0:T(8,128)} %bitcast.3, f32[64,2048]{1,0:T(8,128)} %weight_ref.1, f32[1,65]{1,0:T(1,128)} %bitcast.5), custom_call_target="tpu_custom_call" | custom-call | tf_op jit(solution)/shard_map/pallas_call | solution.py:557
  125.0 0.0 copy-start
  125.0 1.9 %copy.10 = f32[1,64,2048]{2,1,0:T(8,128)} copy(f32[1,64,2048]{2,1,0:T(8,128)} %bitcast.4) | data formatting | bytes 1048576
  127.0 0.0 copy-done
  127.0 0.7 copy.11
Async XLA Ops:
  125.0 1.9 %copy-start = (f32[8,64,64]{2,1,0:T(8,128)S(1)}, f32[8,64,64]{2,1,0:T(8,128)}, u32[]{:S(2)}) copy-start(f32[8,64,64]{2,1,0:T(8,128)} %get-tuple-element.9) | copy-start | bytes 393220

commit v3 on v2

--- a/solution.py
+++ b/solution.py
@@ -361,6 +361,43 @@
 
     sweep(last + 1, 0, 1, finish, None)
 
+    def deal(kind, offset):
+        other, device, own = dealt(offset)
+        part = slice(0, REACH) if kind == 0 else slice(REACH, REACH + 8)
+        return pltpu.make_async_remote_copy(
+            src_ref=out_ref.at[other, part],
+            dst_ref=got_ref.at[held, part],
+            send_sem=deal_send.at[kind, offset],
+            recv_sem=deal_recv.at[kind, offset],
+            device_id=device,
+            device_id_type=MESH,
+        )
+
+    def start_deals(kind):
+        part = slice(0, REACH) if kind == 0 else slice(REACH, REACH + 8)
+
+        def start_deal(offset, carry):
+            other, device, own = dealt(offset)
+
+            @pl.when(jnp.logical_not(own))
+            def _():
+                deal(kind, offset).start()
+
+            @pl.when(own)
+            def _():
+                pltpu.make_async_copy(out_ref.at[other, part], got_ref.at[held, part], deal_recv.at[kind, offset]).start()
+
+            return carry
+
+        lax.fori_loop(0, sims, start_deal, 0)
+
+    def await_deal(offset, carry):
+        for kind in range(2):
+            deal(kind, offset).wait_recv()
+        return carry
+
+    start_deals(0)
+
     zero, one, two, three = (edge_ref[k] for k in range(4))
     gap = jnp.zeros((1, rows), F32)
     before = [jnp.concatenate([gap, x[:-1]], axis=0) for x in (two, three)]
@@ -389,30 +426,7 @@
             out_ref[2 * b, 38:40, :] = rim_in[0, p, 6:8, k * LANES : (k + 1) * LANES]
             out_ref[2 * b + 1, 32:34, :] = rim_in[1, p, 0:2, k * LANES : (k + 1) * LANES]
 
-    def deal(offset):
-        other, device, own = dealt(offset)
-        return pltpu.make_async_remote_copy(
-            src_ref=out_ref.at[other], dst_ref=got_ref.at[held], send_sem=deal_send.at[offset], recv_sem=deal_recv.at[offset], device_id=device, device_id_type=MESH
-        )
-
-    def start_deal(offset, carry):
-        other, device, own = dealt(offset)
-
-        @pl.when(jnp.logical_not(own))
-        def _():
-            deal(offset).start()
-
-        @pl.when(own)
-        def _():
-            pltpu.make_async_copy(out_ref.at[other], got_ref.at[held], deal_recv.at[offset]).start()
-
-        return carry
-
-    def await_deal(offset, carry):
-        deal(offset).wait_recv()
-        return carry
-
-    lax.fori_loop(0, sims, start_deal, 0)
+    start_deals(1)
     for p in range(pairs):
         sent(last, 1, p)
         sent(last + 1, 0, p)
@@ -533,7 +547,8 @@
     def finish_deals(offset, carry):
         @pl.when(jnp.logical_not(dealt(offset)[2]))
         def _():
-            deal(offset).wait_send()
+            for kind in range(2):
+                deal(kind, offset).wait_send()
 
         return carry
 
@@ -587,8 +602,8 @@
             pltpu.SemaphoreType.DMA((2, STEPS, pairs)),
             pltpu.SemaphoreType.DMA((2, pairs)),
             pltpu.SemaphoreType.DMA((2, pairs)),
-            pltpu.SemaphoreType.DMA((sims,)),
-            pltpu.SemaphoreType.DMA((sims,)),
+            pltpu.SemaphoreType.DMA((2, sims)),
+            pltpu.SemaphoreType.DMA((2, sims)),
             pltpu.SemaphoreType.DMA((sims,)),
             pltpu.SemaphoreType.DMA((sims,)),
             pltpu.SemaphoreType.DMA((2, pairs)),

time: 128 us -> 137 us (1.070)
  the two profiles are of different devices: /device:TPU:5 before, /device:TPU:53 now
where the time goes in v3:
time: 137 us
  Pallas kernels  134 us (98%)
  local copies, waits for them, and re-layouts  2.62 us (2%)
    pallas_call x1, Pallas kernels, body(): pl.pallas_call(whole_kernel, out_shape=(jax.ShapeDtypeStruct((rows, cols)...  134 us

profile of v3, /device:TPU:53, one launch (start us, length us, event | category | flops | bytes accessed | tf_op | source)
XLA Modules:
  0.0 136.9 jit_solution(14874157294256266994)
XLA Ops:
  0.6 133.6 %shard_map.77 = (f32[64,2048]{1,0:T(8,128)}, f32[8,64,64]{2,1,0:T(8,128)}) custom-call(s32[32]{0:T(128)} %one_ref.1, s32[32]{0:T(128)} %two_ref.1, s32[32]{0:T(128)} %owner_ref.1, f32[64,2048]{1,0:T(8,128)} %bitcast.3, f32[64,2048]{1,0:T(8,128)} %weight_ref.1, f32[1,65]{1,0:T(1,128)} %bitcast.5), custom_call_target="tpu_custom_call" | custom-call | tf_op jit(solution)/shard_map/pallas_call | solution.py:572
  134.3 0.0 copy-start
  134.3 1.9 %copy.10 = f32[1,64,2048]{2,1,0:T(8,128)} copy(f32[1,64,2048]{2,1,0:T(8,128)} %bitcast.4) | data formatting | bytes 1048576
  136.2 0.0 copy-done
  136.2 0.7 copy.11
Async XLA Ops:
  134.3 1.9 %copy-start = (f32[8,64,64]{2,1,0:T(8,128)S(1)}, f32[8,64,64]{2,1,0:T(8,128)}, u32[]{:S(2)}) copy-start(f32[8,64,64]{2,1,0:T(8,128)} %get-tuple-element.9) | copy-start | bytes 393220

commit v4 on v2

--- a/solution.py
+++ b/solution.py
@@ -395,7 +395,8 @@
             src_ref=out_ref.at[other], dst_ref=got_ref.at[held], send_sem=deal_send.at[offset], recv_sem=deal_recv.at[offset], device_id=device, device_id_type=MESH
         )
 
-    def start_deal(offset, carry):
+    def start_deal(turn, carry):
+        offset = jnp.where(turn % 2 == 1, (turn + 1) // 2, lax.rem(sims - turn // 2, sims))
         other, device, own = dealt(offset)
 
         @pl.when(jnp.logical_not(own))
@@ -461,7 +462,8 @@
             device_id_type=MESH,
         )
 
-    for d in range(sims):
+    order = [(k + 1) // 2 if k % 2 else (sims - k // 2) % sims for k in range(sims)]
+    for d in order:
         s = peer(d)[0]
         f = got_ref[s]
         g = 2.0 * got_ref[one_ref[s]] - got_ref[two_ref[s]]

time: 128 us -> 129 us (level)
  Pallas kernels: 124 us -> 126 us
where the time goes in v4:
time: 129 us
  Pallas kernels  126 us (98%)
  local copies, waits for them, and re-layouts  2.62 us (2%)
    pallas_call x1, Pallas kernels, body(): pl.pallas_call(whole_kernel, out_shape=(jax.ShapeDtypeStruct((rows, cols)...  126 us
    unnamed x4, local copies, waits for them, and re-layouts  2.62 us

profile of v4, /device:TPU:5, one launch (start us, length us, event | category | flops | bytes accessed | tf_op | source)
XLA Modules:
  0.0 128.9 jit_solution(17456379821031871539)
XLA Ops:
  0.6 125.6 %shard_map.77 = (f32[64,2048]{1,0:T(8,128)}, f32[8,64,64]{2,1,0:T(8,128)}) custom-call(s32[32]{0:T(128)} %one_ref.1, s32[32]{0:T(128)} %two_ref.1, s32[32]{0:T(128)} %owner_ref.1, f32[64,2048]{1,0:T(8,128)} %bitcast.3, f32[64,2048]{1,0:T(8,128)} %weight_ref.1, f32[1,65]{1,0:T(1,128)} %bitcast.5), custom_call_target="tpu_custom_call" | custom-call | tf_op jit(solution)/shard_map/pallas_call | solution.py:559
  126.2 0.0 copy-start
  126.3 1.9 %copy.10 = f32[1,64,2048]{2,1,0:T(8,128)} copy(f32[1,64,2048]{2,1,0:T(8,128)} %bitcast.4) | data formatting | bytes 1048576
  128.2 0.0 copy-done
  128.2 0.7 copy.11
Async XLA Ops:
  126.2 1.9 %copy-start = (f32[8,64,64]{2,1,0:T(8,128)S(1)}, f32[8,64,64]{2,1,0:T(8,128)}, u32[]{:S(2)}) copy-start(f32[8,64,64]{2,1,0:T(8,128)} %get-tuple-element.9) | copy-start | bytes 393220
